TPU v7x, 32 devices: a whole 2x2x4 slice. The times are simulated.
32 devices in a mesh: dp: 8 (over z, y), expert: 4 (over x, core).
Axes of the slice: x: 2, y: 2, z: 4, core: 2. Of those that a mesh axis runs over, the one named last changes fastest.
Arguments:
- grad_parts: bfloat16 [8, 12, 704, 2048], P('dp', 'expert'), may hold values from -90 to 90
- momentum: float32 [12, 704, 2048], P('expert', 'dp'), may hold values from -6 to 6
Outputs:
- new_momentum: float32 [12, 704, 2048], P('expert', 'dp')
- muon_update: float32 [12, 704, 2048], P('expert', 'dp')
All inputs are finite; a program needn't handle non-finite values.
Results may differ from a plain program's by a relative error of at most 0.023.
Values may be sent and summed in bfloat16 or wider, within the bound.
No kernel may reach another device: no remote copies, remote signals or barrier semaphores. Data moves between devices by JAX's collectives and lax.ppermute only.
A program may use at most 128 MiB of HBM per device.

v0:
```python
import math
import jax
import jax.numpy as jnp
from jax import lax
from jax.sharding import PartitionSpec as P

NS_ITERS = 3
momentum_decay = 0.95
coef_a = 3.4445
coef_b = -4.775
coef_c = 2.0315


def broadcast(x, axis, root):
    mine = lax.axis_index(axis) == root
    return lax.psum(jnp.where(mine, x, jnp.zeros_like(x)), axis)


def orthogonalize(direction):
    flat = direction.astype(jnp.float32)
    norm_value = jnp.sqrt(jnp.sum(flat * flat))
    current = (flat / (norm_value + 1e-07)).astype(jnp.bfloat16)
    for step in range(NS_ITERS):
        gram = jnp.dot(current, current.T, preferred_element_type=jnp.float32).astype(jnp.bfloat16)
        square = jnp.dot(gram, gram, preferred_element_type=jnp.float32)
        poly = (coef_b * gram.astype(jnp.float32) + coef_c * square).astype(jnp.bfloat16)
        current = (
            coef_a * current.astype(jnp.float32)
            + jnp.dot(poly, current, preferred_element_type=jnp.float32)
        ).astype(jnp.bfloat16)
    return current


def local(grad_parts, momentum):
    partials = grad_parts[0]
    matrix_count = partials.shape[0]
    rows_whole = partials.shape[1]
    columns = partials.shape[2]
    ranks = lax.axis_size("dp")
    stride = ranks // matrix_count
    owner_ranks = [matrix * stride for matrix in range(matrix_count)]
    dp_rank = lax.axis_index("dp")
    summed = lax.psum_scatter(partials, "dp", scatter_dimension=1, tiled=True).astype(jnp.float32)
    shard_rows = summed.shape[1]
    total_sq = lax.psum(jnp.sum(summed * summed), ("dp", "expert"))
    entry_count = matrix_count * lax.axis_size("expert") * rows_whole * columns
    factor = jnp.minimum(1.0, lax.rsqrt(total_sq / entry_count + 1e-06))
    scaled = factor * summed
    new_momentum = momentum_decay * momentum + scaled
    direction = (scaled + momentum_decay * new_momentum).astype(jnp.bfloat16)
    gathered = lax.all_gather(direction, "dp", axis=1, tiled=True)
    selector = jnp.stack([dp_rank == owner for owner in owner_ranks]).astype(jnp.bfloat16)
    owned = jnp.tensordot(selector, gathered, axes=1, preferred_element_type=jnp.float32).astype(
        jnp.bfloat16
    )
    result = orthogonalize(owned)
    blocks_out = []
    for owner in owner_ranks:
        broadcast_full = broadcast(result, "dp", owner)
        blocks_out.append(
            lax.dynamic_slice_in_dim(broadcast_full, dp_rank * shard_rows, shard_rows, 0)
        )
    ortho = jnp.stack(blocks_out)
    muon_update = 0.2 * math.sqrt(max(rows_whole, columns)) * ortho.astype(jnp.float32)
    return (new_momentum, muon_update)


def solution(mesh):
    return jax.shard_map(
        local,
        mesh=mesh,
        in_specs=(P("dp", "expert", None, None), P("expert", "dp", None)),
        out_specs=(P("expert", "dp", None), P("expert", "dp", None)),
        check_vma=False,
    )
```

profile of v0, /device:TPU:0, one launch (start us, length us, event | category | flops | bytes accessed | tf_op | source)
XLA Modules:
  0.0 731.8 jit_solution(7370153273644001469)
XLA Ops:
  7.2 0.0 reduce-scatter.4.cloned.1.call-start
  7.2 13.6 %copy.6 = bf16[3,704,2048]{2,0,1:T(4,128)(2,1)} copy(bf16[3,704,2048]{2,1,0:T(8,128)(2,1)} %bitcast.42) | data formatting | bytes 17301504
  20.8 17.6 %copy.8 = bf16[88,8,3,2048]{3,1,2,0:T(8,128)(2,1)} copy(bf16[88,8,3,2048]{3,2,1,0:T(4,128)(2,1)} %bitcast.38) | data formatting | bytes 17301504
  38.4 0.0 reduce-scatter.4.cloned.1.call-update
  38.4 0.5 all-gather.2.cloned.1.call-start
  38.9 155.8 %reduce-scatter.4.cloned.1.call-done = bf16[88,6144]{1,0:T(8,128)(2,1)} async-done(((bf16[704,6144]{1,0:T(8,128)(2,1)}), bf16[88,6144]{1,0:T(8,128)(2,1)}) %reduce-scatter.4.cloned.1.call-update) | async-done | bytes 1081360
  194.8 3.3 reshape.7
  198.1 1.3 fusion.7
  199.4 39.1 %psum.28 = f32[]{:T(128)} all-reduce(f32[]{:T(128)} %fusion.7), channel_id=1, replica_groups=mesh['dp'=8,'expert'=4] {'dp','expert'}, use_global_device_ids=true, to_apply=%region_2.0 | all-reduce | flops 1 | bytes 8 | tf_op jit(solution)/shard_map/psum | solution.py:45
  239.2 4.4 fusion.6
  243.6 0.0 all-gather.2.cloned.1.call-update
  243.6 0.0 all-reduce.3.cloned.1.call-start
  243.7 128.4 %all-gather.2.cloned.1.call-done = bf16[3,704,2048]{2,1,0:T(8,128)(2,1)} async-done(((bf16[3,88,2048]{2,1,0:T(8,128)(2,1)}), bf16[3,704,2048]{2,1,0:T(8,128)(2,1)}) %all-gather.2.cloned.1.call-update) | async-done | bytes 8650768 | tf_op jit(solution)/shard_map/all_gather | solution.py:51
  372.1 24.8 %fusion = bf16[1,704,2048]{2,0,1:T(2,128)(2,1)S(1)} fusion(bf16[3,704,2048]{2,1,0:T(8,128)(2,1)} %all-gather.2.cloned.1.call-done, pred[1]{0:T(512)(128)(4,1)} %bitcast.3, pred[1]{0:T(512)(128)(4,1)} %bitcast.2, pred[1]{0:T(512)(128)(4,1)} %bitcast.1), kind=kOutput, calls=%fused_computation | convolution fusion | flops 8650758 | bytes 11534339 | tf_op jit(solution)/shard_map/dot_general | solution.py:53
  396.9 0.0 copy-start
  396.9 2.5 copy-done
  399.4 3.4 fusion.2
  403.5 5.0 fusion.3
  408.4 3.4 convolution_convert_fusion.2
  411.8 7.0 add_convert_fusion.2
  418.8 6.1 convolution_convert_fusion.1
  424.9 7.3 add_convert_fusion.1
  432.2 3.4 convolution_convert_fusion
  435.6 9.2 %broadcast_select_fusion.2 = (bf16[704,2048]{1,0:T(8,128)(2,1)}, bf16[704,2048]{1,0:T(8,128)(2,1)}, bf16[704,2048]{1,0:T(8,128)(2,1)}) fusion(pred[]{:T(512)} %eq.12, pred[]{:T(512)} %eq.14, pred[]{:T(512)} %eq.13, bf16[704,2048]{1,0:T(8,128)(2,1)S(1)} %add_convert_fusion.1, bf16[704,704]{1,0:T(8,128)(2,1)} %convolution_convert_fusion), kind=kOutput, calls=%fused_computation.12 | convolution fusion | flops 2740441088 | bytes 12525571 | tf_op jit(solution)/shard_map/dot_general | solution.py:29
  444.7 0.0 all-reduce.3.cloned.1.call-update
  444.8 276.5 %all-reduce.3.cloned.1.call-done = (bf16[704,2048]{1,0:T(8,128)(2,1)}, bf16[704,2048]{1,0:T(8,128)(2,1)}, bf16[704,2048]{1,0:T(8,128)(2,1)}) async-done(((bf16[704,2048]{1,0:T(8,128)(2,1)}, bf16[704,2048]{1,0:T(8,128)(2,1)}, bf16[704,2048]{1,0:T(8,128)(2,1)}), (bf16[704,2048]{1,0:T(8,128)(2,1)}, bf16[704,2048]{1,0:T(8,128)(2,1)}, bf16[704,2048]{1,0:T(8,128)(2,1)})) %all-reduce.3.cloned.1.call-update) | async-done | bytes 8650768 | tf_op jit(solution)/shard_map/psum | solution.py:16
  721.3 1.0 dynamic-slice_bitcast_fusion.2
  722.3 1.2 dynamic-slice_bitcast_fusion
  723.4 1.6 convert_multiply_fusion.3
Async XLA Ops:
  7.2 187.6 %reduce-scatter.4.cloned.1.call-start = ((), (), s32[]{:S(2)}) async-start(), calls=%async_computation.2 | async-start | bytes 9732096
  38.4 333.7 %all-gather.2.cloned.1.call-start = ((), (), s32[]{:S(2)}) async-start(), calls=%async_computation.1 | async-start | bytes 9732096 | tf_op jit(solution)/shard_map/all_gather | solution.py:51
  243.6 477.6 %all-reduce.3.cloned.1.call-start = ((), (), s32[]{:S(2)}) async-start(), calls=%async_computation.3 | async-start | bytes 17301504 | tf_op jit(solution)/shard_map/psum | solution.py:16
  396.9 2.5 copy-start
Sparse Core Ops, SparseCore 0:
  38.5 156.1 reduce-scatter.3
  243.7 128.3 all-gather.1
  444.9 276.3 all-reduce.2
where the time goes:
time: 741 us; the launch traced here: 732 us
  waiting for transfers between devices  561 us (76%)
  matrix products  61.1 us (8%)
  local copies, waits for them, and re-layouts  39.1 us (5%)
  blocking collectives  39.1 us (5%)
  other arithmetic  15.7 us (2%)
  between operations  15.4 us (2%)
    psum x1, waiting for transfers between devices, broadcast(): return lax.psum(jnp.where(mine, x, jnp.zeros_like(x)), axis)  276 us
    unnamed x4, waiting for transfers between devices  156 us
    all_gather x1, waiting for transfers between devices, local(): gathered = lax.all_gather(direction, 'dp', axis=1, tiled=True)  128 us
    psum x1, blocking collectives, local(): total_sq = lax.psum(jnp.sum(summed * summed), ('dp', 'expert'))  39.1 us
    unnamed x5, local copies, waits for them, and re-layouts  36.9 us
    dot_general x1, matrix products, local(): jnp.tensordot(selector, gathered, axes=1, preferred_element_type=jnp.floa...  24.8 us
    dot_general x3, matrix products, orthogonalize(): jnp.dot(poly, current, preferred_element_type=jnp.float32)  23.4 us
  transfers between devices with their start and end apart: 3, of which 3 were waited for; matrix products, arithmetic and copies ran while one was open for 0% of the time, Pallas kernels for 0%

commit v1 on v0

--- a/solution.py
+++ b/solution.py
@@ -3,6 +3,7 @@
 import jax.numpy as jnp
 from jax import lax
 from jax.sharding import PartitionSpec as P
+from jax.lax import all_gather
 
 NS_ITERS = 3
 momentum_decay = 0.95
@@ -11,9 +12,15 @@
 coef_c = 2.0315
 
 
+def _show_axis_part(view, axis_key):
+    a_next = all_gather(view, axis_key)
+    carry_out = jnp.sum(a_next, axis=0)
+    return carry_out
+
+
 def broadcast(x, axis, root):
     mine = lax.axis_index(axis) == root
-    return lax.psum(jnp.where(mine, x, jnp.zeros_like(x)), axis)
+    return _show_axis_part(jnp.where(mine, x, jnp.zeros_like(x)), axis_key=axis)
 
 
 def orthogonalize(direction):

time: 741 us -> 1800 us (2.43)
  waiting for transfers between devices: 561 us -> 1580 us
  other arithmetic: 15.7 us -> 58.6 us
    all_gather x0 -> x3, waiting for transfers between devices: none -> 1300 us  [_show_axis_part(): a_next = all_gather(view, axis_key)]
    psum x1 -> x0, waiting for transfers between devices: 276 us -> none  [broadcast(): return lax.psum(jnp.where(mine, x, jnp.zeros_like(x)), axis)]
    reduce_sum x0 -> x3, other arithmetic: none -> 42.9 us  [_show_axis_part(): carry_out = jnp.sum(a_next, axis=0)]
    unnamed x4 -> x6, waiting for transfers between devices: 156 us -> 157 us
  transfers between devices with their start and end apart: 3 -> 5, of which waited for: 3 -> 5; matrix products, arithmetic and copies ran while one was open for 0% -> 2% of each run, Pallas kernels for 0% -> 0%
where the time goes in v1:
time: 1800 us; the launch traced here: 1790 us
  waiting for transfers between devices  1580 us (88%)
  matrix products  60.6 us (3%)
  other arithmetic  58.6 us (3%)
  blocking collectives  39.1 us (2%)
  local copies, waits for them, and re-layouts  38.1 us (2%)
    all_gather x3, waiting for transfers between devices, _show_axis_part(): a_next = all_gather(view, axis_key)  1300 us
    unnamed x6, waiting for transfers between devices  157 us
    all_gather x1, waiting for transfers between devices, local(): gathered = lax.all_gather(direction, 'dp', axis=1, tiled=True)  128 us
    reduce_sum x3, other arithmetic, _show_axis_part(): carry_out = jnp.sum(a_next, axis=0)  42.9 us
    psum x1, blocking collectives, local(): total_sq = lax.psum(jnp.sum(summed * summed), ('dp', 'expert'))  39.1 us
    unnamed x5, local copies, waits for them, and re-layouts  36.9 us
  transfers between devices with their start and end apart: 5, of which 5 were waited for; matrix products, arithmetic and copies ran while one was open for 2% of the time, Pallas kernels for 0%

profile of v1, /device:TPU:0, one launch (start us, length us, event | category | flops | bytes accessed | tf_op | source)
XLA Modules:
  0.0 1793.0 jit_solution(6982704167929673978)
XLA Ops:
  7.2 13.6 copy.6
  20.8 17.6 copy.8
  38.4 0.5 all-gather.8.cloned.1.call-start
  38.9 155.9 %reduce-scatter.4.cloned.1.call-done = bf16[88,6144]{1,0:T(8,128)(2,1)} async-done(((bf16[704,6144]{1,0:T(8,128)(2,1)}), bf16[88,6144]{1,0:T(8,128)(2,1)}) %reduce-scatter.4.cloned.1.call-update) | async-done | bytes 1081360
  194.8 3.3 reshape.10
  198.1 1.3 fusion.7
  199.4 39.1 %psum.7 = f32[]{:T(128)} all-reduce(f32[]{:T(128)} %fusion.7), channel_id=1, replica_groups=mesh['dp'=8,'expert'=4] {'dp','expert'}, use_global_device_ids=true, to_apply=%region_2.0 | all-reduce | flops 1 | bytes 8 | tf_op jit(solution)/shard_map/psum | solution.py:52
  239.2 4.4 fusion.6
  243.6 0.0 all-gather.10.cloned.1.call-start
  243.7 128.4 %all-gather.8.cloned.1.call-done = bf16[3,704,2048]{2,1,0:T(8,128)(2,1)} async-done(((bf16[3,88,2048]{2,1,0:T(8,128)(2,1)}), bf16[3,704,2048]{2,1,0:T(8,128)(2,1)}) %all-gather.8.cloned.1.call-update) | async-done | bytes 8650768 | tf_op jit(solution)/shard_map/all_gather | solution.py:58
  372.1 24.8 %fusion = bf16[1,704,2048]{2,0,1:T(2,128)(2,1)S(1)} fusion(bf16[3,704,2048]{2,1,0:T(8,128)(2,1)} %all-gather.8.cloned.1.call-done, pred[1]{0:T(512)(128)(4,1)} %bitcast.3, pred[1]{0:T(512)(128)(4,1)} %bitcast.2, pred[1]{0:T(512)(128)(4,1)} %bitcast.1), kind=kOutput, calls=%fused_computation | convolution fusion | flops 8650758 | bytes 11534339 | tf_op jit(solution)/shard_map/dot_general | solution.py:60
  396.9 2.5 copy-done
  399.4 3.4 fusion.2
  403.4 5.0 fusion.3
  408.4 3.4 convolution_convert_fusion.2
  411.8 6.7 add_convert_fusion.2
  418.6 6.1 convolution_convert_fusion.1
  424.7 7.2 add_convert_fusion.1
  431.9 3.4 convolution_convert_fusion
  435.3 9.0 broadcast_select_fusion.2
  444.3 0.0 all-gather.14.cloned.1.call-start
  444.3 0.5 all-gather.14.cloned.1.call-update
  444.8 0.0 all-gather.12.cloned.1.call-start
  444.9 0.5 all-gather.12.cloned.1.call-update
  445.4 438.3 %all-gather.10.cloned.1.call-done = bf16[5632,2048]{1,0:T(8,128)(2,1)} async-done(((bf16[704,2048]{1,0:T(8,128)(2,1)}), bf16[5632,2048]{1,0:T(8,128)(2,1)}) %all-gather.10.cloned.1.call-update) | async-done | bytes 23068688 | tf_op jit(solution)/shard_map/all_gather | solution.py:16
  883.7 13.4 reduce_sum.56
  897.1 429.2 %all-gather.14.cloned.1.call-done = bf16[5632,2048]{1,0:T(8,128)(2,1)} async-done(((bf16[704,2048]{1,0:T(8,128)(2,1)}), bf16[5632,2048]{1,0:T(8,128)(2,1)}) %all-gather.14.cloned.1.call-update) | async-done | bytes 23068688 | tf_op jit(solution)/shard_map/all_gather | solution.py:16
  1326.3 15.0 reduce_sum.58
  1341.3 427.6 %all-gather.12.cloned.1.call-done = bf16[5632,2048]{1,0:T(8,128)(2,1)} async-done(((bf16[704,2048]{1,0:T(8,128)(2,1)}), bf16[5632,2048]{1,0:T(8,128)(2,1)}) %all-gather.12.cloned.1.call-update) | async-done | bytes 23068688 | tf_op jit(solution)/shard_map/all_gather | solution.py:16
  1768.9 14.6 reduce_sum.57
  1783.5 1.2 dynamic-slice_bitcast_fusion
  1784.7 1.6 convert_multiply_fusion.3
  (6 shorter events, 0.1 us)
Async XLA Ops:
  7.2 187.6 %reduce-scatter.4.cloned.1.call-start = ((), (), s32[]{:S(2)}) async-start(), calls=%async_computation.5 | async-start | bytes 9732096
  38.4 333.7 %all-gather.8.cloned.1.call-start = ((), (), s32[]{:S(2)}) async-start(), calls=%async_computation.1 | async-start | bytes 9732096 | tf_op jit(solution)/shard_map/all_gather | solution.py:58
  243.6 640.1 %all-gather.10.cloned.1.call-start = ((), (), s32[]{:S(2)}) async-start(), calls=%async_computation.2 | async-start | bytes 25952256 | tf_op jit(solution)/shard_map/all_gather | solution.py:16
  396.9 2.5 copy-start
  444.3 882.0 %all-gather.14.cloned.1.call-start = ((), (), s32[]{:S(2)}) async-start(), calls=%async_computation.4 | async-start | bytes 25952256 | tf_op jit(solution)/shard_map/all_gather | solution.py:16
  444.8 1324.0 %all-gather.12.cloned.1.call-start = ((), (), s32[]{:S(2)}) async-start(), calls=%async_computation.3 | async-start | bytes 25952256 | tf_op jit(solution)/shard_map/all_gather | solution.py:16
Sparse Core Ops, SparseCore 0:
  38.5 156.2 reduce-scatter.3
  243.7 128.3 all-gather.7
  444.4 439.2 all-gather.9
  885.2 441.0 all-gather.13
  1327.7 441.0 all-gather.11
